TPU v7x, 32 devices: a whole 2x2x4 slice. The times are simulated.
32 devices in a mesh: groups: 2 (over x), tm: 4 (over y, core), chan: 4 (over z).
Axes of the slice: x: 2, y: 2, z: 4, core: 2. Of those that a mesh axis runs over, the one named last changes fastest.
Arguments:
- records: bfloat16 [1536, 1024], P(('groups', 'tm'), 'chan'), parts along dimension 0, may hold values from -6 to 6
- cotangent: bfloat16 [1536, 1024], P(('groups', 'tm'), 'chan'), parts along dimension 0, may hold values from -6 to 6
- filter_weight: bfloat16 [4, 2, 1024, 1024], P(None, None, 'tm', 'chan'), may hold values from -0.125 to 0.125
- gate_weight: bfloat16 [4, 2, 1024, 1024], P(None, None, 'tm', 'chan'), may hold values from -0.125 to 0.125
- mix_weight: bfloat16 [4, 1024, 1024], P(None, 'chan', 'tm'), may hold values from -0.1875 to 0.1875
Outputs:
- output: bfloat16 [1536, 1024], P(('groups', 'tm'), 'chan'), parts along dimension 0
- input_grad: bfloat16 [1536, 1024], P(('groups', 'tm'), 'chan'), parts along dimension 0
There are 2 independent parts, one for each index of `groups`. A program takes and returns all parts, laid end to end along the dimension named above; an argument that names none is the same for every part. Nothing has to cross between parts.
All inputs are finite; a program needn't handle non-finite values.
Results may differ from a plain program's by a relative error of at most 0.018.
Values may be sent and summed in bfloat16 or wider, within the bound.
A program may use at most 64 MiB of HBM per device.

v0:
```python
import jax
import jax.numpy as jnp
from jax import lax
from jax.sharding import PartitionSpec as P


def shifted(shard, axis, by):
    peers = lax.axis_size(axis)
    pairs = [(i, i + by) for i in range(peers) if 0 <= i + by < peers]
    return lax.ppermute(shard, axis, pairs)


def right_product(left, panel):
    return lax.dot_general(
        left, panel, (((1,), (1,)), ((), ())), preferred_element_type=jnp.float32
    )


def local(records, cotangent, filter_weight, gate_weight, mix_weight):
    layer_count = filter_weight.shape[0]
    tm_count = lax.axis_size("tm")
    signal = records
    stored = []
    for layer_index in range(layer_count):
        span_shards = 2**layer_index
        filt_panel, gate_panel, mix_panel = (
            lax.all_gather(filter_weight[layer_index], "tm", axis=1, tiled=True),
            lax.all_gather(gate_weight[layer_index], "tm", axis=1, tiled=True),
            lax.all_gather(mix_weight[layer_index], "tm", axis=1, tiled=True),
        )
        whole_rows = lax.all_gather(signal, "chan", axis=1, tiled=True)
        if span_shards < tm_count:
            earlier = shifted(whole_rows, "tm", span_shards)
        else:
            earlier = jnp.zeros_like(whole_rows)
        pre_filter = jnp.dot(earlier, filt_panel[0], preferred_element_type=jnp.float32) + jnp.dot(
            whole_rows, filt_panel[1], preferred_element_type=jnp.float32
        )
        pre_gate = jnp.dot(earlier, gate_panel[0], preferred_element_type=jnp.float32) + jnp.dot(
            whole_rows, gate_panel[1], preferred_element_type=jnp.float32
        )
        gated = (jnp.tanh(pre_filter) * jax.nn.sigmoid(pre_gate)).astype(jnp.bfloat16)
        mix_term = jnp.dot(gated, mix_panel, preferred_element_type=jnp.float32)
        mixed = lax.psum_scatter(
            mix_term.astype(jnp.bfloat16), "chan", scatter_dimension=1, tiled=True
        ).astype(jnp.float32)
        signal = (signal.astype(jnp.float32) + mixed).astype(jnp.bfloat16)
        stored.append((pre_filter, pre_gate, filt_panel, gate_panel, mix_panel))
    grad_now = cotangent
    for layer_index in reversed(range(layer_count)):
        span_shards = 2**layer_index
        pre_filter, pre_gate, filt_panel, gate_panel, mix_panel = stored[layer_index]
        grad_whole = lax.all_gather(grad_now, "chan", axis=1, tiled=True)
        grad_z = right_product(grad_whole, mix_panel)
        tanh_value = jnp.tanh(pre_filter)
        sig_value = jax.nn.sigmoid(pre_gate)
        grad_filt = (grad_z * sig_value * (1.0 - tanh_value * tanh_value)).astype(jnp.bfloat16)
        grad_gate = (grad_z * tanh_value * sig_value * (1.0 - sig_value)).astype(jnp.bfloat16)
        near_term = right_product(grad_filt, filt_panel[1]) + right_product(
            grad_gate, gate_panel[1]
        )
        far_term = right_product(grad_filt, filt_panel[0]) + right_product(grad_gate, gate_panel[0])
        if span_shards < tm_count:
            advanced = shifted(far_term.astype(jnp.bfloat16), "tm", -span_shards).astype(
                far_term.dtype
            )
        else:
            advanced = jnp.zeros_like(far_term)
        returned = lax.psum_scatter(
            (near_term + advanced).astype(jnp.bfloat16), "chan", scatter_dimension=1, tiled=True
        ).astype(jnp.float32)
        grad_now = (grad_now.astype(jnp.float32) + returned).astype(jnp.bfloat16)
    return (signal, grad_now)


def solution(mesh):
    return jax.shard_map(
        local,
        mesh=mesh,
        in_specs=(
            P(("groups", "tm"), "chan"),
            P(("groups", "tm"), "chan"),
            P(None, None, "tm", "chan"),
            P(None, None, "tm", "chan"),
            P(None, "chan", "tm"),
        ),
        out_specs=(P(("groups", "tm"), "chan"), P(("groups", "tm"), "chan")),
        check_vma=False,
    )
```

profile of v0, /device:TPU:0, one launch (start us, length us, event | category | flops | bytes accessed | tf_op | source)
XLA Modules:
  0.0 409.4 jit_solution(5573307418238194053)
XLA Ops:
  10.7 16.4 %all_gather.60 = bf16[192,1024]{1,0:T(8,128)(2,1)S(1)} all-gather(bf16[192,256]{1,0:T(8,128)(2,1)S(1)} %copy-done.34), channel_id=1, replica_groups=mesh['groups'=2,'tm'=4,'chan'=4] {'chan'}, dimensions={1}, use_global_device_ids=true | all-gather | bytes 491520 | tf_op jit(solution)/shard_map/all_gather | solution.py:31
  29.2 7.7 %all-gather.2 = bf16[1,256,1024]{2,1,0:T(8,128)(2,1)S(1)} all-gather(bf16[1,256,256]{2,1,0:T(8,128)(2,1)S(1)} %get-tuple-element.14), channel_id=4, replica_groups=mesh['groups'=2,'tm'=4,'chan'=4] {'tm'}, dimensions={2}, use_global_device_ids=true | all-gather | bytes 655360 | tf_op jit(solution)/shard_map/all_gather | solution.py:29
  38.3 9.2 %all-gather.23.cloned.1.call-done = bf16[1,2,1024,256]{3,2,1,0:T(8,128)(2,1)} async-done(((bf16[1,2,256,256]{3,2,1,0:T(8,128)(2,1)}), bf16[1,2,1024,256]{3,2,1,0:T(8,128)(2,1)}) %all-gather.23.cloned.1.call-update) | async-done | bytes 1048592 | tf_op jit(solution)/shard_map/all_gather | solution.py:28
  54.1 7.2 %all-gather.5 = bf16[1,256,1024]{2,1,0:T(8,128)(2,1)S(1)} all-gather(bf16[1,256,256]{2,1,0:T(8,128)(2,1)S(1)} %get-tuple-element.15), channel_id=7, replica_groups=mesh['groups'=2,'tm'=4,'chan'=4] {'tm'}, dimensions={2}, use_global_device_ids=true | all-gather | bytes 655360 | tf_op jit(solution)/shard_map/all_gather | solution.py:29
  61.3 11.6 %reduce-scatter.9.cloned.1.call-done = bf16[192,256]{1,0:T(8,128)(2,1)} async-done(((bf16[192,1024]{1,0:T(8,128)(2,1)}), bf16[192,256]{1,0:T(8,128)(2,1)}) %reduce-scatter.9.cloned.1.call-update) | async-done | bytes 98320 | tf_op jit(solution)/shard_map/reduce_scatter | solution.py:44
  73.9 14.3 %all_gather.64 = bf16[192,1024]{1,0:T(8,128)(2,1)S(1)} all-gather(bf16[192,256]{1,0:T(8,128)(2,1)S(1)} %add_convert_fusion.9), channel_id=1, replica_groups=mesh['groups'=2,'tm'=4,'chan'=4] {'chan'}, dimensions={1}, use_global_device_ids=true | all-gather | bytes 491520 | tf_op jit(solution)/shard_map/all_gather | solution.py:31
  88.2 4.1 %collective-permute-start.1 = (bf16[192,1024]{1,0:T(8,128)(2,1)S(1)}, bf16[192,1024]{1,0:T(8,128)(2,1)}, u32[]{:S(2)}, u32[]{:S(2)}) collective-permute-start(bf16[192,1024]{1,0:T(8,128)(2,1)S(1)} %all_gather.64), channel_id=1, source_target_pairs={{0,8},{4,12},{1,9},{5,13},{2,10},{6,14},{3,11},{7,15},{16,24},{20,... | collective-permute-start | bytes 1179656 | tf_op jit(solution)/shard_map/ppermute | solution.py:10
  94.4 14.1 %all-gather.27.cloned.1.call-done = bf16[1,2,1024,256]{3,2,1,0:T(8,128)(2,1)} async-done(((bf16[1,2,256,256]{3,2,1,0:T(8,128)(2,1)}), bf16[1,2,1024,256]{3,2,1,0:T(8,128)(2,1)}) %all-gather.27.cloned.1.call-update) | async-done | bytes 1048592 | tf_op jit(solution)/shard_map/all_gather | solution.py:28
  116.1 10.4 %all-gather.11 = bf16[1,256,1024]{2,1,0:T(8,128)(2,1)S(1)} all-gather(bf16[1,256,256]{2,1,0:T(8,128)(2,1)S(1)} %copy-done.33), channel_id=13, replica_groups=mesh['groups'=2,'tm'=4,'chan'=4] {'tm'}, dimensions={2}, use_global_device_ids=true | all-gather | bytes 655360 | tf_op jit(solution)/shard_map/all_gather | solution.py:29
  126.5 7.3 %all-gather.8 = bf16[1,256,1024]{2,1,0:T(8,128)(2,1)S(1)} all-gather(bf16[1,256,256]{2,1,0:T(8,128)(2,1)S(1)} %copy-done.32), channel_id=10, replica_groups=mesh['groups'=2,'tm'=4,'chan'=4] {'tm'}, dimensions={2}, use_global_device_ids=true | all-gather | bytes 655360 | tf_op jit(solution)/shard_map/all_gather | solution.py:29
  135.8 12.0 %all-gather.31.cloned.1.call-done = bf16[1,2,1024,256]{3,2,1,0:T(8,128)(2,1)} async-done(((bf16[1,2,256,256]{3,2,1,0:T(8,128)(2,1)}), bf16[1,2,1024,256]{3,2,1,0:T(8,128)(2,1)}) %all-gather.31.cloned.1.call-update) | async-done | bytes 1048592 | tf_op jit(solution)/shard_map/all_gather | solution.py:28
  149.8 21.1 %reduce-scatter.11.cloned.1.call-done = bf16[192,256]{1,0:T(8,128)(2,1)} async-done(((bf16[192,1024]{1,0:T(8,128)(2,1)}), bf16[192,256]{1,0:T(8,128)(2,1)}) %reduce-scatter.11.cloned.1.call-update) | async-done | bytes 98320 | tf_op jit(solution)/shard_map/reduce_scatter | solution.py:44
  171.9 14.3 %all_gather.69 = bf16[192,1024]{1,0:T(8,128)(2,1)S(1)} all-gather(bf16[192,256]{1,0:T(8,128)(2,1)S(1)} %add_convert_fusion.8), channel_id=1, replica_groups=mesh['groups'=2,'tm'=4,'chan'=4] {'chan'}, dimensions={1}, use_global_device_ids=true | all-gather | bytes 491520 | tf_op jit(solution)/shard_map/all_gather | solution.py:31
  189.9 14.8 %all_gather.76 = bf16[192,1024]{1,0:T(8,128)(2,1)S(1)} all-gather(bf16[192,256]{1,0:T(8,128)(2,1)S(1)} %copy-done.35), channel_id=1, replica_groups=mesh['groups'=2,'tm'=4,'chan'=4] {'chan'}, dimensions={1}, use_global_device_ids=true | all-gather | bytes 491520 | tf_op jit(solution)/shard_map/all_gather | solution.py:53
  209.8 18.9 %reduce-scatter.13.cloned.1.call-done = bf16[192,256]{1,0:T(8,128)(2,1)} async-done(((bf16[192,1024]{1,0:T(8,128)(2,1)}), bf16[192,256]{1,0:T(8,128)(2,1)}) %reduce-scatter.13.cloned.1.call-update) | async-done | bytes 98320 | tf_op jit(solution)/shard_map/reduce_scatter | solution.py:44
  230.3 14.3 %all_gather.73 = bf16[192,1024]{1,0:T(8,128)(2,1)S(1)} all-gather(bf16[192,256]{1,0:T(8,128)(2,1)S(1)} %add_convert_fusion.7), channel_id=1, replica_groups=mesh['groups'=2,'tm'=4,'chan'=4] {'chan'}, dimensions={1}, use_global_device_ids=true | all-gather | bytes 491520 | tf_op jit(solution)/shard_map/all_gather | solution.py:31
  249.2 19.7 %reduce-scatter.17.cloned.1.call-done = bf16[192,256]{1,0:T(8,128)(2,1)} async-done(((bf16[192,1024]{1,0:T(8,128)(2,1)}), bf16[192,256]{1,0:T(8,128)(2,1)}) %reduce-scatter.17.cloned.1.call-update) | async-done | bytes 98320 | tf_op jit(solution)/shard_map/reduce_scatter | solution.py:69
  270.7 14.3 %all_gather.77 = bf16[192,1024]{1,0:T(8,128)(2,1)S(1)} all-gather(bf16[192,256]{1,0:T(8,128)(2,1)S(1)} %add_convert_fusion.5), channel_id=1, replica_groups=mesh['groups'=2,'tm'=4,'chan'=4] {'chan'}, dimensions={1}, use_global_device_ids=true | all-gather | bytes 491520 | tf_op jit(solution)/shard_map/all_gather | solution.py:53
  288.2 19.6 %reduce-scatter.19.cloned.1.call-done = bf16[192,256]{1,0:T(8,128)(2,1)} async-done(((bf16[192,1024]{1,0:T(8,128)(2,1)}), bf16[192,256]{1,0:T(8,128)(2,1)}) %reduce-scatter.19.cloned.1.call-update) | async-done | bytes 98320 | tf_op jit(solution)/shard_map/reduce_scatter | solution.py:69
  308.8 14.4 %all_gather.78 = bf16[192,1024]{1,0:T(8,128)(2,1)S(1)} all-gather(bf16[192,256]{1,0:T(8,128)(2,1)S(1)} %add_convert_fusion.4), channel_id=1, replica_groups=mesh['groups'=2,'tm'=4,'chan'=4] {'chan'}, dimensions={1}, use_global_device_ids=true | all-gather | bytes 491520 | tf_op jit(solution)/shard_map/all_gather | solution.py:53
  326.8 8.0 %collective-permute-done.2 = bf16[192,1024]{1,0:T(8,128)(2,1)S(1)} collective-permute-done((bf16[192,1024]{1,0:T(8,128)(2,1)S(1)}, bf16[192,1024]{1,0:T(8,128)(2,1)S(1)}, u32[]{:S(2)}, u32[]{:S(2)}) %collective-permute-start.2) | collective-permute-done | bytes 393248 | tf_op jit(solution)/shard_map/ppermute | solution.py:10
  337.9 16.8 %reduce-scatter.21.cloned.1.call-done = bf16[192,256]{1,0:T(8,128)(2,1)} async-done(((bf16[192,1024]{1,0:T(8,128)(2,1)}), bf16[192,256]{1,0:T(8,128)(2,1)}) %reduce-scatter.21.cloned.1.call-update) | async-done | bytes 98320 | tf_op jit(solution)/shard_map/reduce_scatter | solution.py:69
  355.7 16.2 %all_gather.79 = bf16[192,1024]{1,0:T(8,128)(2,1)S(1)} all-gather(bf16[192,256]{1,0:T(8,128)(2,1)S(1)} %add_convert_fusion.3), channel_id=1, replica_groups=mesh['groups'=2,'tm'=4,'chan'=4] {'chan'}, dimensions={1}, use_global_device_ids=true | all-gather | bytes 491520 | tf_op jit(solution)/shard_map/all_gather | solution.py:53
  381.0 20.3 %reduce-scatter.23.cloned.1.call-done = bf16[192,256]{1,0:T(8,128)(2,1)} async-done(((bf16[192,1024]{1,0:T(8,128)(2,1)}), bf16[192,256]{1,0:T(8,128)(2,1)}) %reduce-scatter.23.cloned.1.call-update) | async-done | bytes 98320 | tf_op jit(solution)/shard_map/reduce_scatter | solution.py:69
  (173 shorter events, 68.0 us)
Async XLA Ops:
  7.2 29.7 %all-gather.21.cloned.1.call-start = ((), (), s32[]{:S(2)}) async-start(), calls=%async_computation.16 | async-start | bytes 1310720 | tf_op jit(solution)/shard_map/all_gather | solution.py:27
  9.6 37.9 %all-gather.23.cloned.1.call-start = ((), (), s32[]{:S(2)}) async-start(), calls=%async_computation.17 | async-start | bytes 1310720 | tf_op jit(solution)/shard_map/all_gather | solution.py:28
  10.6 17.8 %copy-start.31 = (bf16[4,256,256]{2,1,0:T(8,128)(2,1)S(1)}, bf16[4,256,256]{2,1,0:T(8,128)(2,1)}, u32[]{:S(2)}) copy-start(bf16[4,256,256]{2,1,0:T(8,128)(2,1)} %param.9) | copy-start | bytes 1572868
  10.7 62.3 %reduce-scatter.9.cloned.1.call-start = ((), (), s32[]{:S(2)}) async-start(), calls=%async_computation.8 | async-start | bytes 491520 | tf_op jit(solution)/shard_map/reduce_scatter | solution.py:44
  27.1 21.7 %collective-permute-start = (bf16[192,1024]{1,0:T(8,128)(2,1)S(1)}, bf16[192,1024]{1,0:T(8,128)(2,1)S(1)}, u32[]{:S(2)}, u32[]{:S(2)}) collective-permute-start(bf16[192,1024]{1,0:T(8,128)(2,1)S(1)} %all_gather.60), channel_id=1, source_target_pairs={{0,4},{4,8},{8,12},{1,5},{5,9},{9,13},{2,6},{6,10},{10,14},{3,7},{... | collective-permute-start | bytes 1179656 | tf_op jit(solution)/shard_map/ppermute | solution.py:10
  51.6 40.7 %all-gather.25.cloned.1.call-start = ((), (), s32[]{:S(2)}) async-start(), calls=%async_computation.18 | async-start | bytes 1310720 | tf_op jit(solution)/shard_map/all_gather | solution.py:27
  52.2 56.3 %all-gather.27.cloned.1.call-start = ((), (), s32[]{:S(2)}) async-start(), calls=%async_computation.19 | async-start | bytes 1310720 | tf_op jit(solution)/shard_map/all_gather | solution.py:28
  52.8 81.0 %all-gather.29.cloned.1.call-start = ((), (), s32[]{:S(2)}) async-start(), calls=%async_computation.20 | async-start | bytes 1310720 | tf_op jit(solution)/shard_map/all_gather | solution.py:27
  53.3 94.4 %all-gather.31.cloned.1.call-start = ((), (), s32[]{:S(2)}) async-start(), calls=%async_computation.21 | async-start | bytes 1310720 | tf_op jit(solution)/shard_map/all_gather | solution.py:28
  54.1 116.8 %reduce-scatter.11.cloned.1.call-start = ((), (), s32[]{:S(2)}) async-start(), calls=%async_computation.9 | async-start | bytes 491520 | tf_op jit(solution)/shard_map/reduce_scatter | solution.py:44
  88.2 21.7 %collective-permute-start.1 = (bf16[192,1024]{1,0:T(8,128)(2,1)S(1)}, bf16[192,1024]{1,0:T(8,128)(2,1)}, u32[]{:S(2)}, u32[]{:S(2)}) collective-permute-start(bf16[192,1024]{1,0:T(8,128)(2,1)S(1)} %all_gather.64), channel_id=1, source_target_pairs={{0,8},{4,12},{1,9},{5,13},{2,10},{6,14},{3,11},{7,15},{16,24},{20,... | collective-permute-start | bytes 1179656 | tf_op jit(solution)/shard_map/ppermute | solution.py:10
  114.4 91.3 %all-gather.33.cloned.1.call-start = ((), (), s32[]{:S(2)}) async-start(), calls=%async_computation.22 | async-start | bytes 1310720 | tf_op jit(solution)/shard_map/all_gather | solution.py:27
  115.2 92.6 %all-gather.35.cloned.1.call-start = ((), (), s32[]{:S(2)}) async-start(), calls=%async_computation.23 | async-start | bytes 1310720 | tf_op jit(solution)/shard_map/all_gather | solution.py:28
  115.8 112.9 %reduce-scatter.13.cloned.1.call-start = ((), (), s32[]{:S(2)}) async-start(), calls=%async_computation.10 | async-start | bytes 491520 | tf_op jit(solution)/shard_map/reduce_scatter | solution.py:44
  135.8 35.1 %copy-start.22 = (bf16[192,256]{1,0:T(8,128)(2,1)S(1)}, bf16[192,256]{1,0:T(8,128)(2,1)}, u32[]{:S(2)}) copy-start(bf16[192,256]{1,0:T(8,128)(2,1)} %copy-done.21) | copy-start | bytes 294916
  189.0 79.9 %reduce-scatter.17.cloned.1.call-start = ((), (), s32[]{:S(2)}) async-start(), calls=%async_computation.12 | async-start | bytes 491520 | tf_op jit(solution)/shard_map/reduce_scatter | solution.py:69
  207.7 20.9 %copy-start.24 = (bf16[192,256]{1,0:T(8,128)(2,1)S(1)}, bf16[192,256]{1,0:T(8,128)(2,1)}, u32[]{:S(2)}) copy-start(bf16[192,256]{1,0:T(8,128)(2,1)} %copy-done.23) | copy-start | bytes 294916
  249.2 58.7 %reduce-scatter.19.cloned.1.call-start = ((), (), s32[]{:S(2)}) async-start(), calls=%async_computation.13 | async-start | bytes 491520 | tf_op jit(solution)/shard_map/reduce_scatter | solution.py:69
  288.1 19.7 %copy-start.26 = (bf16[192,256]{1,0:T(8,128)(2,1)S(1)}, bf16[192,256]{1,0:T(8,128)(2,1)}, u32[]{:S(2)}) copy-start(bf16[192,256]{1,0:T(8,128)(2,1)} %copy-done.25) | copy-start | bytes 294916
  288.2 66.6 %reduce-scatter.21.cloned.1.call-start = ((), (), s32[]{:S(2)}) async-start(), calls=%async_computation.14 | async-start | bytes 491520 | tf_op jit(solution)/shard_map/reduce_scatter | solution.py:69
  325.1 9.7 %collective-permute-start.2 = (bf16[192,1024]{1,0:T(8,128)(2,1)S(1)}, bf16[192,1024]{1,0:T(8,128)(2,1)S(1)}, u32[]{:S(2)}, u32[]{:S(2)}) collective-permute-start(bf16[192,1024]{1,0:T(8,128)(2,1)S(1)} %fusion.2), channel_id=1, source_target_pairs={{8,0},{12,4},{9,1},{13,5},{10,2},{14,6},{11,3},{15,7},{24,16},{28,... | collective-permute-start | bytes 1179656 | tf_op jit(solution)/shard_map/ppermute | solution.py:10
  335.9 42.7 %reduce-scatter.15.cloned.1.call-start = ((), (), s32[]{:S(2)}) async-start(), calls=%async_computation.11 | async-start | bytes 491520 | tf_op jit(solution)/shard_map/reduce_scatter | solution.py:44
  337.9 63.5 %reduce-scatter.23.cloned.1.call-start = ((), (), s32[]{:S(2)}) async-start(), calls=%async_computation.15 | async-start | bytes 491520 | tf_op jit(solution)/shard_map/reduce_scatter | solution.py:69
  373.8 3.6 collective-permute-start.3
  (37 other events, 224.7 us)
Sparse Core Ops, SparseCore 0:
  9.7 19.4 all-gather.20
  30.7 16.6 all-gather.22
  51.7 21.1 reduce-scatter.8
  74.3 14.9 all-gather.24
  90.8 17.6 all-gather.26
  109.9 19.4 all-gather.28
  131.0 16.6 all-gather.30
  150.0 20.7 reduce-scatter.10
  172.4 14.9 all-gather.32
  188.8 16.6 all-gather.34
  207.8 20.7 reduce-scatter.12
  249.3 19.6 reduce-scatter.16
  288.3 19.5 reduce-scatter.18
  336.0 18.6 reduce-scatter.20
  356.9 19.8 reduce-scatter.14
  378.9 22.3 reduce-scatter.22
where the time goes:
time: 411 us; the launch traced here: 409 us
  waiting for transfers between devices  177 us (43%)
  blocking collectives  151 us (37%)
  matrix products  34.2 us (8%)
  local copies, waits for them, and re-layouts  14.6 us (4%)
  between operations  14.4 us (4%)
  other arithmetic  8.99 us (2%)
  starting transfers between devices  8.64 us (2%)
    reduce_scatter x4, waiting for transfers between devices, local(): lax.psum_scatter((near_term + advanced).astype(jnp.bfloat16), 'chan', sca...  76.5 us
    all_gather x4, blocking collectives, local(): grad_whole = lax.all_gather(grad_now, 'chan', axis=1, tiled=True)  59.7 us
    all_gather x4, blocking collectives, local(): whole_rows = lax.all_gather(signal, 'chan', axis=1, tiled=True)  59.3 us
    reduce_scatter x4, waiting for transfers between devices, local(): lax.psum_scatter(mix_term.astype(jnp.bfloat16), 'chan', scatter_dimension...  51.7 us
    all_gather x4, waiting for transfers between devices, local(): lax.all_gather(gate_weight[layer_index], 'tm', axis=1, tiled=True)  35.2 us
    all_gather x4, blocking collectives, local(): lax.all_gather(mix_weight[layer_index], 'tm', axis=1, tiled=True)  32.4 us
    unnamed x82, local copies, waits for them, and re-layouts  10.6 us
    ppermute x4, waiting for transfers between devices, shifted(): return lax.ppermute(shard, axis, pairs)  10 us
  transfers between devices with their start and end apart: 20, of which 12 were waited for; matrix products, arithmetic and copies ran while one was open for 8% of the time, Pallas kernels for 0%

commit v1 on v0

--- a/solution.py
+++ b/solution.py
@@ -2,6 +2,16 @@
 import jax.numpy as jnp
 from jax import lax
 from jax.sharding import PartitionSpec as P
+
+
+def pass_along(x, axis, d):
+    size = lax.axis_size(axis)
+    moving, parts = (x, [x])
+    for _ in range(size - 1):
+        moving = lax.ppermute(moving, axis, [(i, (i + 1) % size) for i in range(size)])
+        parts.insert(0, moving)
+    merged = jnp.concatenate(parts, axis=d)
+    return jnp.roll(merged, (lax.axis_index(axis) + 1) * x.shape[d], axis=d)
 
 
 def shifted(shard, axis, by):
@@ -28,7 +38,7 @@
             lax.all_gather(gate_weight[layer_index], "tm", axis=1, tiled=True),
             lax.all_gather(mix_weight[layer_index], "tm", axis=1, tiled=True),
         )
-        whole_rows = lax.all_gather(signal, "chan", axis=1, tiled=True)
+        whole_rows = pass_along(signal, "chan", 1)
         if span_shards < tm_count:
             earlier = shifted(whole_rows, "tm", span_shards)
         else:

time: 411 us -> 410 us (level)
  blocking collectives: 151 us -> 91.2 us
  waiting for transfers between devices: 177 us -> 227 us
  starting transfers between devices: 8.64 us -> 17.2 us
    all_gather x4 -> x0, blocking collectives: 59.3 us -> none  [local(): whole_rows = lax.all_gather(signal, 'chan', axis=1, tiled=True)]
    ppermute x0 -> x12, waiting for transfers between devices: none -> 27.7 us  [pass_along(): lax.ppermute(moving, axis, [(i, (i + 1) % size) for i in range(size)])]
    all_gather x4, waiting for transfers between devices: 35.2 us -> 49.7 us  [local(): lax.all_gather(gate_weight[layer_index], 'tm', axis=1, tiled=True)]
    all_gather x4, waiting for transfers between devices: 0.01 us -> 12.2 us  [local(): lax.all_gather(filter_weight[layer_index], 'tm', axis=1, tiled=True)]
    ppermute x0 -> x12, starting transfers between devices: none -> 8.24 us  [pass_along(): lax.ppermute(moving, axis, [(i, (i + 1) % size) for i in range(size)])]
    reduce_scatter x4, waiting for transfers between devices: 51.7 us -> 44.9 us  [local(): lax.psum_scatter(mix_term.astype(jnp.bfloat16), 'chan', scatter_dimension...]
    all_gather x4, blocking collectives: 32.4 us -> 27.8 us  [local(): lax.all_gather(mix_weight[layer_index], 'tm', axis=1, tiled=True)]
  transfers between devices with their start and end apart: 20 -> 32, of which waited for: 12 -> 20; matrix products, arithmetic and copies ran while one was open for 8% -> 6% of each run, Pallas kernels for 0% -> 0%
where the time goes in v1:
time: 410 us; the launch traced here: 408 us
  waiting for transfers between devices  227 us (55%)
  blocking collectives  91.2 us (22%)
  matrix products  30.9 us (8%)
  starting transfers between devices  17.2 us (4%)
  local copies, waits for them, and re-layouts  15.1 us (4%)
  between operations  14.5 us (4%)
  other arithmetic  11.9 us (3%)
    reduce_scatter x4, waiting for transfers between devices, local(): lax.psum_scatter((near_term + advanced).astype(jnp.bfloat16), 'chan', sca...  78.2 us
    all_gather x4, blocking collectives, local(): grad_whole = lax.all_gather(grad_now, 'chan', axis=1, tiled=True)  63.4 us
    all_gather x4, waiting for transfers between devices, local(): lax.all_gather(gate_weight[layer_index], 'tm', axis=1, tiled=True)  49.7 us
    reduce_scatter x4, waiting for transfers between devices, local(): lax.psum_scatter(mix_term.astype(jnp.bfloat16), 'chan', scatter_dimension...  44.9 us
    all_gather x4, blocking collectives, local(): lax.all_gather(mix_weight[layer_index], 'tm', axis=1, tiled=True)  27.8 us
    ppermute x12, waiting for transfers between devices, pass_along(): lax.ppermute(moving, axis, [(i, (i + 1) % size) for i in range(size)])  27.7 us
    all_gather x4, waiting for transfers between devices, local(): lax.all_gather(filter_weight[layer_index], 'tm', axis=1, tiled=True)  12.2 us
    unnamed x82, local copies, waits for them, and re-layouts  11 us
  transfers between devices with their start and end apart: 32, of which 20 were waited for; matrix products, arithmetic and copies ran while one was open for 6% of the time, Pallas kernels for 0%

profile of v1, /device:TPU:0, one launch (start us, length us, event | category | flops | bytes accessed | tf_op | source)
XLA Modules:
  0.0 408.3 jit_solution(4011157352912723473)
XLA Ops:
  20.1 5.7 %collective-permute-done.1 = bf16[192,256]{1,0:T(8,128)(2,1)S(1)} collective-permute-done((bf16[192,256]{1,0:T(8,128)(2,1)S(1)}, bf16[192,256]{1,0:T(8,128)(2,1)S(1)}, u32[]{:S(2)}, u32[]{:S(2)}) %collective-permute-start.1) | collective-permute-done | bytes 98336 | tf_op jit(solution)/shard_map/ppermute | solution.py:11
  25.8 7.2 %all-gather.2 = bf16[1,256,1024]{2,1,0:T(8,128)(2,1)S(1)} all-gather(bf16[1,256,256]{2,1,0:T(8,128)(2,1)S(1)} %get-tuple-element.15), channel_id=4, replica_groups=mesh['groups'=2,'tm'=4,'chan'=4] {'tm'}, dimensions={2}, use_global_device_ids=true | all-gather | bytes 655360 | tf_op jit(solution)/shard_map/all_gather | solution.py:39
  37.3 10.1 %all-gather.23.cloned.1.call-done = bf16[1,2,1024,256]{3,2,1,0:T(8,128)(2,1)} async-done(((bf16[1,2,256,256]{3,2,1,0:T(8,128)(2,1)}), bf16[1,2,1024,256]{3,2,1,0:T(8,128)(2,1)}) %all-gather.23.cloned.1.call-update) | async-done | bytes 1048592 | tf_op jit(solution)/shard_map/all_gather | solution.py:38
  52.8 22.7 %reduce-scatter.9.cloned.1.call-done = bf16[192,256]{1,0:T(8,128)(2,1)} async-done(((bf16[192,1024]{1,0:T(8,128)(2,1)}), bf16[192,256]{1,0:T(8,128)(2,1)}) %reduce-scatter.9.cloned.1.call-update) | async-done | bytes 98320 | tf_op jit(solution)/shard_map/reduce_scatter | solution.py:54
  76.4 6.4 %collective-permute-done.4 = bf16[192,256]{1,0:T(8,128)(2,1)S(1)} collective-permute-done((bf16[192,256]{1,0:T(8,128)(2,1)S(1)}, bf16[192,256]{1,0:T(8,128)(2,1)S(1)}, u32[]{:S(2)}, u32[]{:S(2)}) %collective-permute-start.4) | collective-permute-done | bytes 98336 | tf_op jit(solution)/shard_map/ppermute | solution.py:11
  82.8 6.7 %collective-permute-done.5 = bf16[192,256]{1,0:T(8,128)(2,1)S(1)} collective-permute-done((bf16[192,256]{1,0:T(8,128)(2,1)S(1)}, bf16[192,256]{1,0:T(8,128)(2,1)S(1)}, u32[]{:S(2)}, u32[]{:S(2)}) %collective-permute-start.5) | collective-permute-done | bytes 98336 | tf_op jit(solution)/shard_map/ppermute | solution.py:11
  89.5 7.1 %all-gather.5 = bf16[1,256,1024]{2,1,0:T(8,128)(2,1)S(1)} all-gather(bf16[1,256,256]{2,1,0:T(8,128)(2,1)S(1)} %get-tuple-element.16), channel_id=7, replica_groups=mesh['groups'=2,'tm'=4,'chan'=4] {'tm'}, dimensions={2}, use_global_device_ids=true | all-gather | bytes 655360 | tf_op jit(solution)/shard_map/all_gather | solution.py:39
  102.7 9.4 %all-gather.27.cloned.1.call-done = bf16[1,2,1024,256]{3,2,1,0:T(8,128)(2,1)} async-done(((bf16[1,2,256,256]{3,2,1,0:T(8,128)(2,1)}), bf16[1,2,1024,256]{3,2,1,0:T(8,128)(2,1)}) %all-gather.27.cloned.1.call-update) | async-done | bytes 1048592 | tf_op jit(solution)/shard_map/all_gather | solution.py:38
  120.4 22.2 %reduce-scatter.11.cloned.1.call-done = bf16[192,256]{1,0:T(8,128)(2,1)} async-done(((bf16[192,1024]{1,0:T(8,128)(2,1)}), bf16[192,256]{1,0:T(8,128)(2,1)}) %reduce-scatter.11.cloned.1.call-update) | async-done | bytes 98320 | tf_op jit(solution)/shard_map/reduce_scatter | solution.py:54
  143.6 7.0 %all-gather.8 = bf16[1,256,1024]{2,1,0:T(8,128)(2,1)S(1)} all-gather(bf16[1,256,256]{2,1,0:T(8,128)(2,1)S(1)} %copy-done.34), channel_id=10, replica_groups=mesh['groups'=2,'tm'=4,'chan'=4] {'tm'}, dimensions={2}, use_global_device_ids=true | all-gather | bytes 655360 | tf_op jit(solution)/shard_map/all_gather | solution.py:39
  151.8 7.2 %all-gather.29.cloned.1.call-done = bf16[1,2,1024,256]{3,2,1,0:T(8,128)(2,1)} async-done(((bf16[1,2,256,256]{3,2,1,0:T(8,128)(2,1)}), bf16[1,2,1024,256]{3,2,1,0:T(8,128)(2,1)}) %all-gather.29.cloned.1.call-update) | async-done | bytes 1048592 | tf_op jit(solution)/shard_map/all_gather | solution.py:37
  161.9 15.4 %all-gather.31.cloned.1.call-done = bf16[1,2,1024,256]{3,2,1,0:T(8,128)(2,1)} async-done(((bf16[1,2,256,256]{3,2,1,0:T(8,128)(2,1)}), bf16[1,2,1024,256]{3,2,1,0:T(8,128)(2,1)}) %all-gather.31.cloned.1.call-update) | async-done | bytes 1048592 | tf_op jit(solution)/shard_map/all_gather | solution.py:38
  183.6 18.8 %all_gather.60 = bf16[192,1024]{1,0:T(8,128)(2,1)} all-gather(bf16[192,256]{1,0:T(8,128)(2,1)S(1)} %copy-done.36), channel_id=1, replica_groups=mesh['groups'=2,'tm'=4,'chan'=4] {'chan'}, dimensions={1}, use_global_device_ids=true | all-gather | bytes 491520 | tf_op jit(solution)/shard_map/all_gather | solution.py:63
  202.4 6.5 %all-gather.11 = bf16[1,256,1024]{2,1,0:T(8,128)(2,1)S(1)} all-gather(bf16[1,256,256]{2,1,0:T(8,128)(2,1)S(1)} %copy-done.33), channel_id=13, replica_groups=mesh['groups'=2,'tm'=4,'chan'=4] {'tm'}, dimensions={2}, use_global_device_ids=true | all-gather | bytes 655360 | tf_op jit(solution)/shard_map/all_gather | solution.py:39
  216.7 5.0 %all-gather.33.cloned.1.call-done = bf16[1,2,1024,256]{3,2,1,0:T(8,128)(2,1)} async-done(((bf16[1,2,256,256]{3,2,1,0:T(8,128)(2,1)}), bf16[1,2,1024,256]{3,2,1,0:T(8,128)(2,1)}) %all-gather.33.cloned.1.call-update) | async-done | bytes 1048592 | tf_op jit(solution)/shard_map/all_gather | solution.py:37
  225.2 14.8 %all-gather.35.cloned.1.call-done = bf16[1,2,1024,256]{3,2,1,0:T(8,128)(2,1)} async-done(((bf16[1,2,256,256]{3,2,1,0:T(8,128)(2,1)}), bf16[1,2,1024,256]{3,2,1,0:T(8,128)(2,1)}) %all-gather.35.cloned.1.call-update) | async-done | bytes 1048592 | tf_op jit(solution)/shard_map/all_gather | solution.py:38
  246.1 20.9 %reduce-scatter.17.cloned.1.call-done = bf16[192,256]{1,0:T(8,128)(2,1)} async-done(((bf16[192,1024]{1,0:T(8,128)(2,1)}), bf16[192,256]{1,0:T(8,128)(2,1)}) %reduce-scatter.17.cloned.1.call-update) | async-done | bytes 98320 | tf_op jit(solution)/shard_map/reduce_scatter | solution.py:79
  268.7 14.3 %all_gather.61 = bf16[192,1024]{1,0:T(8,128)(2,1)S(1)} all-gather(bf16[192,256]{1,0:T(8,128)(2,1)S(1)} %add_convert_fusion.5), channel_id=1, replica_groups=mesh['groups'=2,'tm'=4,'chan'=4] {'chan'}, dimensions={1}, use_global_device_ids=true | all-gather | bytes 491520 | tf_op jit(solution)/shard_map/all_gather | solution.py:63
  286.3 19.8 %reduce-scatter.19.cloned.1.call-done = bf16[192,256]{1,0:T(8,128)(2,1)} async-done(((bf16[192,1024]{1,0:T(8,128)(2,1)}), bf16[192,256]{1,0:T(8,128)(2,1)}) %reduce-scatter.19.cloned.1.call-update) | async-done | bytes 98320 | tf_op jit(solution)/shard_map/reduce_scatter | solution.py:79
  307.7 14.6 %all_gather.62 = bf16[192,1024]{1,0:T(8,128)(2,1)S(1)} all-gather(bf16[192,256]{1,0:T(8,128)(2,1)S(1)} %add_convert_fusion.4), channel_id=1, replica_groups=mesh['groups'=2,'tm'=4,'chan'=4] {'chan'}, dimensions={1}, use_global_device_ids=true | all-gather | bytes 491520 | tf_op jit(solution)/shard_map/all_gather | solution.py:63
  325.8 8.0 %collective-permute-done.14 = bf16[192,1024]{1,0:T(8,128)(2,1)S(1)} collective-permute-done((bf16[192,1024]{1,0:T(8,128)(2,1)S(1)}, bf16[192,1024]{1,0:T(8,128)(2,1)S(1)}, u32[]{:S(2)}, u32[]{:S(2)}) %collective-permute-start.14) | collective-permute-done | bytes 393248 | tf_op jit(solution)/shard_map/ppermute | solution.py:20
  336.9 16.6 %reduce-scatter.21.cloned.1.call-done = bf16[192,256]{1,0:T(8,128)(2,1)} async-done(((bf16[192,1024]{1,0:T(8,128)(2,1)}), bf16[192,256]{1,0:T(8,128)(2,1)}) %reduce-scatter.21.cloned.1.call-update) | async-done | bytes 98320 | tf_op jit(solution)/shard_map/reduce_scatter | solution.py:79
  354.5 15.8 %all_gather.63 = bf16[192,1024]{1,0:T(8,128)(2,1)S(1)} all-gather(bf16[192,256]{1,0:T(8,128)(2,1)S(1)} %add_convert_fusion.3), channel_id=1, replica_groups=mesh['groups'=2,'tm'=4,'chan'=4] {'chan'}, dimensions={1}, use_global_device_ids=true | all-gather | bytes 491520 | tf_op jit(solution)/shard_map/all_gather | solution.py:63
  379.4 20.9 %reduce-scatter.23.cloned.1.call-done = bf16[192,256]{1,0:T(8,128)(2,1)} async-done(((bf16[192,1024]{1,0:T(8,128)(2,1)}), bf16[192,256]{1,0:T(8,128)(2,1)}) %reduce-scatter.23.cloned.1.call-update) | async-done | bytes 98320 | tf_op jit(solution)/shard_map/reduce_scatter | solution.py:79
  (197 shorter events, 90.8 us)
Async XLA Ops:
  7.2 28.6 %all-gather.21.cloned.1.call-start = ((), (), s32[]{:S(2)}) async-start(), calls=%async_computation.16 | async-start | bytes 1310720 | tf_op jit(solution)/shard_map/all_gather | solution.py:37
  9.5 37.9 %all-gather.23.cloned.1.call-start = ((), (), s32[]{:S(2)}) async-start(), calls=%async_computation.17 | async-start | bytes 1310720 | tf_op jit(solution)/shard_map/all_gather | solution.py:38
  10.6 64.8 %reduce-scatter.9.cloned.1.call-start = ((), (), s32[]{:S(2)}) async-start(), calls=%async_computation.8 | async-start | bytes 491520 | tf_op jit(solution)/shard_map/reduce_scatter | solution.py:54
  11.5 7.9 %collective-permute-start = (bf16[192,256]{1,0:T(8,128)(2,1)S(1)}, bf16[192,256]{1,0:T(8,128)(2,1)S(1)}, u32[]{:S(2)}, u32[]{:S(2)}) collective-permute-start(bf16[192,256]{1,0:T(8,128)(2,1)S(1)} %copy-done.35), channel_id=1, source_target_pairs={{0,1},{1,2},{2,3},{3,0},{4,5},{5,6},{6,7},{7,4},{8,9},{9,10},{10,1... | collective-permute-start | bytes 294920 | tf_op jit(solution)/shard_map/ppermute | solution.py:11
  25.8 7.2 %collective-permute-start.2 = (bf16[192,256]{1,0:T(8,128)(2,1)S(1)}, bf16[192,256]{1,0:T(8,128)(2,1)S(1)}, u32[]{:S(2)}, u32[]{:S(2)}) collective-permute-start(bf16[192,256]{1,0:T(8,128)(2,1)S(1)} %collective-permute-done.1), channel_id=1, source_target_pairs={{0,1},{1,2},{2,3},{3,0},{4,5},{5,6},{6,7},{7,4},{8,9},{9,10},{10,1... | collective-permute-start | bytes 294920 | tf_op jit(solution)/shard_map/ppermute | solution.py:11
  33.5 15.3 %collective-permute-start.3 = (bf16[192,1024]{1,0:T(8,128)(2,1)S(1)}, bf16[192,1024]{1,0:T(8,128)(2,1)S(1)}, u32[]{:S(2)}, u32[]{:S(2)}) collective-permute-start(bf16[192,1024]{1,0:T(8,128)(2,1)S(1)} %fusion.74), channel_id=1, source_target_pairs={{0,4},{4,8},{8,12},{1,5},{5,9},{9,13},{2,6},{6,10},{10,14},{3,7},{... | collective-permute-start | bytes 1179656 | tf_op jit(solution)/shard_map/ppermute | solution.py:20
  51.5 49.1 %all-gather.25.cloned.1.call-start = ((), (), s32[]{:S(2)}) async-start(), calls=%async_computation.18 | async-start | bytes 1310720 | tf_op jit(solution)/shard_map/all_gather | solution.py:37
  52.1 60.0 %all-gather.27.cloned.1.call-start = ((), (), s32[]{:S(2)}) async-start(), calls=%async_computation.19 | async-start | bytes 1310720 | tf_op jit(solution)/shard_map/all_gather | solution.py:38
  52.7 89.9 %reduce-scatter.11.cloned.1.call-start = ((), (), s32[]{:S(2)}) async-start(), calls=%async_computation.9 | async-start | bytes 491520 | tf_op jit(solution)/shard_map/reduce_scatter | solution.py:54
  97.2 17.2 %collective-permute-start.7 = (bf16[192,1024]{1,0:T(8,128)(2,1)S(1)}, bf16[192,1024]{1,0:T(8,128)(2,1)}, u32[]{:S(2)}, u32[]{:S(2)}) collective-permute-start(bf16[192,1024]{1,0:T(8,128)(2,1)S(1)} %fusion.67), channel_id=1, source_target_pairs={{0,8},{4,12},{1,9},{5,13},{2,10},{6,14},{3,11},{7,15},{16,24},{20,... | collective-permute-start | bytes 1179656 | tf_op jit(solution)/shard_map/ppermute | solution.py:20
  118.8 40.2 %all-gather.29.cloned.1.call-start = ((), (), s32[]{:S(2)}) async-start(), calls=%async_computation.20 | async-start | bytes 1310720 | tf_op jit(solution)/shard_map/all_gather | solution.py:37
  119.6 57.8 %all-gather.31.cloned.1.call-start = ((), (), s32[]{:S(2)}) async-start(), calls=%async_computation.21 | async-start | bytes 1310720 | tf_op jit(solution)/shard_map/all_gather | solution.py:38
  120.3 88.5 %reduce-scatter.13.cloned.1.call-start = ((), (), s32[]{:S(2)}) async-start(), calls=%async_computation.10 | async-start | bytes 491520 | tf_op jit(solution)/shard_map/reduce_scatter | solution.py:54
  150.6 9.8 %collective-permute-start.9 = (bf16[192,256]{1,0:T(8,128)(2,1)S(1)}, bf16[192,256]{1,0:T(8,128)(2,1)S(1)}, u32[]{:S(2)}, u32[]{:S(2)}) collective-permute-start(bf16[192,256]{1,0:T(8,128)(2,1)S(1)} %collective-permute-done.8), channel_id=1, source_target_pairs={{0,1},{1,2},{2,3},{3,0},{4,5},{5,6},{6,7},{7,4},{8,9},{9,10},{10,1... | collective-permute-start | bytes 294920 | tf_op jit(solution)/shard_map/ppermute | solution.py:11
  160.4 18.4 %collective-permute-start.10 = (bf16[192,256]{1,0:T(8,128)(2,1)S(1)}, bf16[192,256]{1,0:T(8,128)(2,1)S(1)}, u32[]{:S(2)}, u32[]{:S(2)}) collective-permute-start(bf16[192,256]{1,0:T(8,128)(2,1)S(1)} %collective-permute-done.9), channel_id=1, source_target_pairs={{0,1},{1,2},{2,3},{3,0},{4,5},{5,6},{6,7},{7,4},{8,9},{9,10},{10,1... | collective-permute-start | bytes 294920 | tf_op jit(solution)/shard_map/ppermute | solution.py:11
  182.0 39.7 %all-gather.33.cloned.1.call-start = ((), (), s32[]{:S(2)}) async-start(), calls=%async_computation.22 | async-start | bytes 1310720 | tf_op jit(solution)/shard_map/all_gather | solution.py:37
  182.6 57.4 %all-gather.35.cloned.1.call-start = ((), (), s32[]{:S(2)}) async-start(), calls=%async_computation.23 | async-start | bytes 1310720 | tf_op jit(solution)/shard_map/all_gather | solution.py:38
  183.3 83.6 %reduce-scatter.17.cloned.1.call-start = ((), (), s32[]{:S(2)}) async-start(), calls=%async_computation.12 | async-start | bytes 491520 | tf_op jit(solution)/shard_map/reduce_scatter | solution.py:79
  223.7 17.7 %collective-permute-start.13 = (bf16[192,256]{1,0:T(8,128)(2,1)}, bf16[192,256]{1,0:T(8,128)(2,1)}, u32[]{:S(2)}, u32[]{:S(2)}) collective-permute-start(bf16[192,256]{1,0:T(8,128)(2,1)} %collective-permute-done.12), channel_id=1, source_target_pairs={{0,1},{1,2},{2,3},{3,0},{4,5},{5,6},{6,7},{7,4},{8,9},{9,10},{10,1... | collective-permute-start | bytes 294920 | tf_op jit(solution)/shard_map/ppermute | solution.py:11
  246.0 60.0 %reduce-scatter.19.cloned.1.call-start = ((), (), s32[]{:S(2)}) async-start(), calls=%async_computation.13 | async-start | bytes 491520 | tf_op jit(solution)/shard_map/reduce_scatter | solution.py:79
  286.2 67.4 %reduce-scatter.21.cloned.1.call-start = ((), (), s32[]{:S(2)}) async-start(), calls=%async_computation.14 | async-start | bytes 491520 | tf_op jit(solution)/shard_map/reduce_scatter | solution.py:79
  324.1 9.7 %collective-permute-start.14 = (bf16[192,1024]{1,0:T(8,128)(2,1)S(1)}, bf16[192,1024]{1,0:T(8,128)(2,1)S(1)}, u32[]{:S(2)}, u32[]{:S(2)}) collective-permute-start(bf16[192,1024]{1,0:T(8,128)(2,1)S(1)} %fusion.2), channel_id=1, source_target_pairs={{8,0},{12,4},{9,1},{13,5},{10,2},{14,6},{11,3},{15,7},{24,16},{28,... | collective-permute-start | bytes 1179656 | tf_op jit(solution)/shard_map/ppermute | solution.py:20
  334.9 42.0 %reduce-scatter.15.cloned.1.call-start = ((), (), s32[]{:S(2)}) async-start(), calls=%async_computation.11 | async-start | bytes 491520 | tf_op jit(solution)/shard_map/reduce_scatter | solution.py:54
  336.9 63.3 %reduce-scatter.23.cloned.1.call-start = ((), (), s32[]{:S(2)}) async-start(), calls=%async_computation.15 | async-start | bytes 491520 | tf_op jit(solution)/shard_map/reduce_scatter | solution.py:79
  (49 other events, 370.6 us)
Sparse Core Ops, SparseCore 0:
  9.6 19.4 all-gather.20
  30.7 16.6 all-gather.22
  51.7 23.7 reduce-scatter.8
  76.8 14.9 all-gather.24
  93.2 18.8 all-gather.26
  118.9 23.6 reduce-scatter.10
  144.2 14.8 all-gather.28
  160.6 16.6 all-gather.30
  182.1 22.2 reduce-scatter.12
  205.9 15.7 all-gather.32
  223.3 16.6 all-gather.34
  246.1 20.7 reduce-scatter.16
  286.3 19.6 reduce-scatter.18
  335.1 18.4 reduce-scatter.20
  355.7 19.9 reduce-scatter.14
  377.8 22.3 reduce-scatter.22
